TPU v7x, 256 devices: a whole 4x4x8 slice. The times are simulated.
256 devices in a mesh: row: 16 (over y, x), col: 16 (over z, core).
Axes of the slice: x: 4, y: 4, z: 8, core: 2. Of those that a mesh axis runs over, the one named last changes fastest.
Arguments:
- block_values: float32 [16, 16, 40, 128, 128], P('row', 'col'), may hold values from 7.8125e-06 to 0.00078125
- block_index: int32 [16, 16, 2, 40], P('row', 'col'), may hold values from 0 to 31, as said below
- block_count: int32 [16, 16], P('row', 'col'), may hold values from 1 to 40, as said below
- strength: float32 [32], replicated, may hold values from 1 to 30
- raw_scores: float32 [512, 32, 128], P(('row', 'col')), may hold values from -24 to 24
Outputs:
- smoothed: float32 [512, 32, 128], P(('row', 'col'))
- final_residual: float32 [512, 32, 128], P(('row', 'col'))
Inputs may be any that keep to these rules, and one draw needn't show every extreme that they name: `block_count`: some device has exactly 40 live slots; the others hold between half and all of their share of the upper triangle, scaled to 40. `block_index`: the live slots of one device name distinct blocks, each with global block row at most its global block column; slots at or above the count hold pairs in range that are ignored.
All inputs are finite; a program needn't handle non-finite values.
Results may differ from a plain program's by a relative error of at most 0.0003.
Values sent between devices are 32-bit elements; how exact they have to be, the bound alone decides.
A program may use at most 64 MiB of HBM per device.

v0:
```python
import jax
import jax.numpy as jnp
from jax import lax
from jax.sharding import PartitionSpec as P

ITERS = 3


def local_terms(values, row_index, col_index, panel_rows, panel_cols):
    picked_cols = jnp.take(panel_cols, col_index, axis=0)
    picked_rows = jnp.take(panel_rows, row_index, axis=0)
    to_rows = jnp.einsum("crk,cik->cri", picked_cols, values, precision=lax.Precision.HIGHEST)
    to_cols = jnp.einsum("cri,cik->crk", picked_rows, values, precision=lax.Precision.HIGHEST)
    row_part = jax.ops.segment_sum(to_rows, row_index, num_segments=panel_rows.shape[0])
    col_part = jax.ops.segment_sum(to_cols, col_index, num_segments=panel_cols.shape[0])
    return (row_part, col_part)


def fold_terms(row_part, col_part):
    return lax.psum_scatter(row_part, "col", scatter_dimension=0, tiled=True) + lax.psum_scatter(
        col_part, "row", scatter_dimension=0, tiled=True
    )


def total(field):
    return jnp.sum(field, axis=(0, 2))


def global_sum(partial_sum):
    return lax.psum(partial_sum, ("row", "col"))


def shards(block_values, block_index, block_count, strength, raw_scores):
    values = block_values[0, 0]
    row_index = block_index[0, 0, 0]
    col_index = block_index[0, 0, 1]
    live_mask = (jnp.arange(values.shape[0], dtype=jnp.int32) < block_count[0, 0]).astype(
        jnp.float32
    )
    masked = values * live_mask[:, None, None]
    segment = raw_scores.shape[0]
    block_size = raw_scores.shape[2]
    rows_here = lax.axis_size("col") * segment
    cols_here = lax.axis_size("row") * segment
    ones_rows = jnp.ones((rows_here, 1, block_size), jnp.float32)
    ones_cols = jnp.ones((cols_here, 1, block_size), jnp.float32)
    degree_rows, degree_cols = local_terms(masked, row_index, col_index, ones_rows, ones_cols)
    degree = fold_terms(degree_rows, degree_cols)
    gains = strength[None, :, None]
    smoothed = jnp.zeros_like(raw_scores)
    residual = raw_scores
    direction = raw_scores
    norm_now = global_sum(total(residual * residual))
    for iteration in range(ITERS):
        panel_rows = lax.all_gather(direction, "col", axis=0, tiled=True)
        panel_cols = lax.all_gather(direction, "row", axis=0, tiled=True)
        row_part, col_part = local_terms(masked, row_index, col_index, panel_rows, panel_cols)
        product = fold_terms(row_part, col_part)
        image = direction + gains * (degree * direction - product)
        step_size = norm_now / global_sum(total(direction * image))
        smoothed = smoothed + step_size[None, :, None] * direction
        residual = residual - step_size[None, :, None] * image
        norm_next = global_sum(total(residual * residual))
        direction = residual + (norm_next / norm_now)[None, :, None] * direction
        norm_now = norm_next
    return (smoothed, residual)


def solution(mesh):
    placed = (
        P("row", "col", None, None, None),
        P("row", "col", None, None),
        P("row", "col"),
        P(),
        P(("row", "col"), None, None),
    )
    return jax.shard_map(
        shards,
        mesh=mesh,
        in_specs=placed,
        out_specs=(P(("row", "col"), None, None), P(("row", "col"), None, None)),
        check_vma=False,
    )
```

profile of v0, /device:TPU:1, one launch (start us, length us, event | category | flops | bytes accessed | tf_op | source)
XLA Modules:
  0.0 916.9 jit_solution(5695150841030016190)
XLA Ops:
  9.4 23.0 %all_gather.19 = f32[32,32,128]{2,1,0:T(8,128)S(1)} all-gather(f32[2,32,128]{2,1,0:T(8,128)} %param.13), channel_id=1, replica_groups=mesh['row'=16,'col'=16] {'col'}, dimensions={0}, use_global_device_ids=true | all-gather | bytes 557056 | tf_op jit(solution)/shard_map/all_gather | solution.py:55
  33.0 5.0 fusion.4
  38.1 4.9 scatter_fusion.1
  43.9 19.6 %all_gather.18 = f32[32,32,128]{2,1,0:T(8,128)S(1)} all-gather(f32[2,32,128]{2,1,0:T(8,128)S(1)} %copy-done.7), channel_id=1, replica_groups=mesh['row'=16,'col'=16] {'row'}, dimensions={0}, use_global_device_ids=true | all-gather | bytes 557056 | tf_op jit(solution)/shard_map/all_gather | solution.py:56
  64.9 6.2 fusion.5
  71.1 4.7 scatter_fusion
  88.7 58.4 %all-reduce.1 = f32[32,1,128]{2,0,1:T(8,128)S(1)} all-reduce(f32[32,1,128]{2,0,1:T(8,128)S(1)} %bitcast.49), channel_id=3, replica_groups=mesh['row'=16,'col'=16] {'row'}, use_global_device_ids=true, to_apply=%region_5.7.clone | all-reduce | flops 4096 | bytes 32768
  147.1 61.3 %all-reduce = f32[32,1,128]{2,0,1:T(8,128)S(1)} all-reduce(f32[32,1,128]{2,0,1:T(8,128)S(1)} %bitcast.48), channel_id=2, replica_groups=mesh['row'=16,'col'=16] {'col'}, use_global_device_ids=true, to_apply=%region_3.5.clone | all-reduce | flops 4096 | bytes 32768
  209.5 74.0 %all-reduce.2 = (f32[32]{0:T(128)S(1)}, f32[32]{0:T(128)S(1)}) all-reduce(f32[32]{0:T(128)S(1)} %get-tuple-element.5, f32[32]{0:T(128)S(1)} %get-tuple-element.4), channel_id=1, replica_groups=mesh['row'=16,'col'=16] {'row','col'}, use_global_device_ids=true, to_apply=%region_1.2 | all-reduce | flops 64 | bytes 512 | tf_op jit(solution)/shard_map/psum | solution.py:30
  284.5 74.5 %psum.44 = f32[32]{0:T(128)S(1)} all-reduce(f32[32]{0:T(128)S(1)} %get-tuple-element.10), channel_id=1, replica_groups=mesh['row'=16,'col'=16] {'row','col'}, use_global_device_ids=true, to_apply=%region_13.16 | all-reduce | flops 32 | bytes 256 | tf_op jit(solution)/shard_map/psum | solution.py:30
  359.0 17.2 %all_gather.21 = f32[32,32,128]{2,1,0:T(8,128)S(1)} all-gather(f32[2,32,128]{2,1,0:T(8,128)S(1)} %multiply_add_fusion.4), channel_id=1, replica_groups=mesh['row'=16,'col'=16] {'col'}, dimensions={0}, use_global_device_ids=true | all-gather | bytes 557056 | tf_op jit(solution)/shard_map/all_gather | solution.py:55
  387.7 19.2 %all_gather.20 = f32[32,32,128]{2,1,0:T(8,128)S(1)} all-gather(f32[2,32,128]{2,1,0:T(8,128)S(1)} %multiply_add_fusion.4), channel_id=1, replica_groups=mesh['row'=16,'col'=16] {'row'}, dimensions={0}, use_global_device_ids=true | all-gather | bytes 557056 | tf_op jit(solution)/shard_map/all_gather | solution.py:56
  408.3 6.2 fusion.3
  414.5 4.7 scatter_fusion.2
  420.1 38.4 %reduce-scatter.15.cloned.1.call-done = f32[2,32,128]{2,1,0:T(8,128)} async-done(((f32[32,32,128]{2,1,0:T(8,128)}), f32[2,32,128]{2,1,0:T(8,128)}) %reduce-scatter.15.cloned.1.call-update) | async-done | bytes 32784 | tf_op jit(solution)/shard_map/reduce_scatter | solution.py:20
  458.5 57.2 %reduce-scatter.13.cloned.1.call-done = f32[2,32,128]{2,1,0:T(8,128)} async-done(((f32[32,32,128]{2,1,0:T(8,128)}), f32[2,32,128]{2,1,0:T(8,128)}) %reduce-scatter.13.cloned.1.call-update) | async-done | bytes 32784 | tf_op jit(solution)/shard_map/reduce_scatter | solution.py:20
  516.7 79.6 %psum.45 = f32[32]{0:T(128)S(1)} all-reduce(f32[32]{0:T(128)S(1)} %multiply_reduce_fusion.2), channel_id=1, replica_groups=mesh['row'=16,'col'=16] {'row','col'}, use_global_device_ids=true, to_apply=%region_19.22 | all-reduce | flops 32 | bytes 256 | tf_op jit(solution)/shard_map/psum | solution.py:30
  597.2 72.4 %psum.46 = f32[32]{0:T(128)S(1)} all-reduce(f32[32]{0:T(128)S(1)} %get-tuple-element.8), channel_id=1, replica_groups=mesh['row'=16,'col'=16] {'row','col'}, use_global_device_ids=true, to_apply=%region_21.24 | all-reduce | flops 32 | bytes 256 | tf_op jit(solution)/shard_map/psum | solution.py:30
  669.6 18.1 %all_gather.23 = f32[32,32,128]{2,1,0:T(8,128)S(1)} all-gather(f32[2,32,128]{2,1,0:T(8,128)S(1)} %multiply_add_fusion.2), channel_id=1, replica_groups=mesh['row'=16,'col'=16] {'col'}, dimensions={0}, use_global_device_ids=true | all-gather | bytes 557056 | tf_op jit(solution)/shard_map/all_gather | solution.py:55
  699.1 19.2 %all_gather.22 = f32[32,32,128]{2,1,0:T(8,128)S(1)} all-gather(f32[2,32,128]{2,1,0:T(8,128)S(1)} %multiply_add_fusion.2), channel_id=1, replica_groups=mesh['row'=16,'col'=16] {'row'}, dimensions={0}, use_global_device_ids=true | all-gather | bytes 557056 | tf_op jit(solution)/shard_map/all_gather | solution.py:56
  719.8 5.3 fusion.1
  728.7 41.8 %reduce-scatter.19.cloned.1.call-done = f32[2,32,128]{2,1,0:T(8,128)} async-done(((f32[32,32,128]{2,1,0:T(8,128)}), f32[2,32,128]{2,1,0:T(8,128)}) %reduce-scatter.19.cloned.1.call-update) | async-done | bytes 32784 | tf_op jit(solution)/shard_map/reduce_scatter | solution.py:20
  770.5 57.3 %reduce-scatter.17.cloned.1.call-done = f32[2,32,128]{2,1,0:T(8,128)} async-done(((f32[32,32,128]{2,1,0:T(8,128)}), f32[2,32,128]{2,1,0:T(8,128)}) %reduce-scatter.17.cloned.1.call-update) | async-done | bytes 32784 | tf_op jit(solution)/shard_map/reduce_scatter | solution.py:20
  828.8 79.8 %psum.47 = f32[32]{0:T(128)S(1)} all-reduce(f32[32]{0:T(128)S(1)} %multiply_reduce_fusion), channel_id=1, replica_groups=mesh['row'=16,'col'=16] {'row','col'}, use_global_device_ids=true, to_apply=%region_27.30 | all-reduce | flops 32 | bytes 256 | tf_op jit(solution)/shard_map/psum | solution.py:30
  (82 shorter events, 52.6 us)
Async XLA Ops:
  7.2 201.3 %reduce-scatter.11.cloned.1.call-start = ((), (), s32[]{:S(2)}) async-start(), calls=%async_computation.7 | async-start | bytes 557056 | tf_op jit(solution)/shard_map/reduce_scatter | solution.py:20
  33.0 10.9 %copy-start.7 = (f32[2,32,128]{2,1,0:T(8,128)S(1)}, f32[2,32,128]{2,1,0:T(8,128)}, u32[]{:S(2)}) copy-start(f32[2,32,128]{2,1,0:T(8,128)} %param.13) | copy-start | bytes 98308
  38.0 26.9 %copy-start = (f32[1,1,40,128,128]{4,3,2,1,0:T(8,128)S(1)}, f32[1,1,40,128,128]{4,3,2,1,0:T(8,128)}, u32[]{:S(2)}) copy-start(f32[1,1,40,128,128]{4,3,2,1,0:T(8,128)} %param.9) | copy-start | bytes 7864324
  42.9 0.8 copy-start.3
  43.8 164.7 %reduce-scatter.9.cloned.1.call-start = ((), (), s32[]{:S(2)}) async-start(), calls=%async_computation.6 | async-start | bytes 557056 | tf_op jit(solution)/shard_map/reduce_scatter | solution.py:20
  71.1 6.8 copy-start.10
  71.1 7.4 copy-start.9
  75.8 0.8 copy-start.4
  76.7 381.8 %reduce-scatter.15.cloned.1.call-start = ((), (), s32[]{:S(2)}) async-start(), calls=%async_computation.9 | async-start | bytes 557056 | tf_op jit(solution)/shard_map/reduce_scatter | solution.py:20
  80.4 128.1 %copy-start.8 = (f32[32]{0:T(128)S(1)}, f32[32]{0:T(128)}, u32[]{:S(2)}) copy-start(f32[32]{0:T(128)} %param.12) | copy-start | bytes 388
  386.8 0.8 copy-start.5
  387.6 128.1 %reduce-scatter.13.cloned.1.call-start = ((), (), s32[]{:S(2)}) async-start(), calls=%async_computation.8 | async-start | bytes 557056 | tf_op jit(solution)/shard_map/reduce_scatter | solution.py:20
  419.2 0.8 copy-start.6
  420.0 350.5 %reduce-scatter.19.cloned.1.call-start = ((), (), s32[]{:S(2)}) async-start(), calls=%async_computation.11 | async-start | bytes 557056 | tf_op jit(solution)/shard_map/reduce_scatter | solution.py:20
  698.3 0.8 copy-start.2
  699.1 128.7 %reduce-scatter.17.cloned.1.call-start = ((), (), s32[]{:S(2)}) async-start(), calls=%async_computation.10 | async-start | bytes 557056 | tf_op jit(solution)/shard_map/reduce_scatter | solution.py:20
  727.9 0.8 copy-start.1
Sparse Core Ops, SparseCore 0:
  43.9 73.4 reduce-scatter.10
  120.0 55.2 reduce-scatter.8
  387.7 70.6 reduce-scatter.14
  461.0 54.6 reduce-scatter.12
  699.2 71.2 reduce-scatter.18
  773.0 54.7 reduce-scatter.16
where the time goes:
time: 918 us; the launch traced here: 917 us
  blocking collectives  616 us (67%)
  waiting for transfers between devices  195 us (21%)
  matrix products  37.9 us (4%)
  other arithmetic  35.4 us (4%)
  between operations  16.3 us (2%)
  local copies, waits for them, and re-layouts  15.9 us (2%)
    psum x5, blocking collectives, global_sum(): return lax.psum(partial_sum, ('row', 'col'))  380 us
    unnamed x2, blocking collectives  120 us
    reduce_scatter x3, waiting for transfers between devices, fold_terms(): lax.psum_scatter(row_part, 'col', scatter_dimension=0, tiled=True)  115 us
    reduce_scatter x3, waiting for transfers between devices, fold_terms(): lax.psum_scatter(col_part, 'row', scatter_dimension=0, tiled=True)  80.2 us
    all_gather x3, blocking collectives, shards(): panel_rows = lax.all_gather(direction, 'col', axis=0, tiled=True)  58.3 us
    all_gather x3, blocking collectives, shards(): panel_cols = lax.all_gather(direction, 'row', axis=0, tiled=True)  58 us
    dot_general x4, matrix products, local_terms(): jnp.einsum('crk,cik->cri', picked_cols, values, precision=lax.Precision.H...  22 us
  transfers between devices with their start and end apart: 6, of which 4 were waited for; matrix products, arithmetic and copies ran while one was open for 5% of the time, Pallas kernels for 0%

commit v1 on v0

--- a/solution.py
+++ b/solution.py
@@ -27,7 +27,7 @@
 
 
 def global_sum(partial_sum):
-    return lax.psum(partial_sum, ("row", "col"))
+    return jnp.sum(lax.all_gather(partial_sum, ("row", "col")), axis=0)
 
 
 def shards(block_values, block_index, block_count, strength, raw_scores):

time: 918 us -> 1080 us (1.18)
  waiting for transfers between devices: 195 us -> 430 us
  blocking collectives: 616 us -> 541 us
    psum x5 -> x0, blocking collectives: 380 us -> none  [global_sum(): return lax.psum(partial_sum, ('row', 'col'))]
    unnamed x2 -> x6, blocking collectives: 120 us -> 427 us
    unnamed x6 -> x8, waiting for transfers between devices: 0.1 us -> 234 us
  transfers between devices with their start and end apart: 6 -> 7, of which waited for: 4 -> 5; matrix products, arithmetic and copies ran while one was open for 5% -> 4% of each run, Pallas kernels for 0% -> 0%
where the time goes in v1:
time: 1080 us
  blocking collectives  541 us (50%)
  waiting for transfers between devices  430 us (40%)
  matrix products  37.9 us (4%)
  other arithmetic  35.7 us (3%)
  local copies, waits for them, and re-layouts  20.2 us (2%)
  between operations  16.5 us (2%)
    unnamed x6, blocking collectives  427 us
    unnamed x8, waiting for transfers between devices  234 us
    reduce_scatter x3, waiting for transfers between devices, fold_terms(): lax.psum_scatter(row_part, 'col', scatter_dimension=0, tiled=True)  115 us
    reduce_scatter x3, waiting for transfers between devices, fold_terms(): lax.psum_scatter(col_part, 'row', scatter_dimension=0, tiled=True)  81.4 us
    all_gather x3, blocking collectives, shards(): panel_rows = lax.all_gather(direction, 'col', axis=0, tiled=True)  59.5 us
    all_gather x3, blocking collectives, shards(): panel_cols = lax.all_gather(direction, 'row', axis=0, tiled=True)  55.4 us
    dot_general x4, matrix products, local_terms(): jnp.einsum('crk,cik->cri', picked_cols, values, precision=lax.Precision.H...  22 us
  transfers between devices with their start and end apart: 7, of which 5 were waited for; matrix products, arithmetic and copies ran while one was open for 4% of the time, Pallas kernels for 0%

profile of v1, /device:TPU:1, one launch (start us, length us, event | category | flops | bytes accessed | tf_op | source)
XLA Modules:
  0.0 1082.4 jit_solution(5773921166962846330)
XLA Ops:
  9.4 23.0 %all_gather.57 = f32[32,32,128]{2,1,0:T(8,128)S(1)} all-gather(f32[2,32,128]{2,1,0:T(8,128)} %param.13), channel_id=1, replica_groups=mesh['row'=16,'col'=16] {'col'}, dimensions={0}, use_global_device_ids=true | all-gather | bytes 557056 | tf_op jit(solution)/shard_map/all_gather | solution.py:55
  33.0 5.0 fusion.4
  38.1 4.9 scatter_fusion.1
  43.9 19.6 %all_gather.56 = f32[32,32,128]{2,1,0:T(8,128)S(1)} all-gather(f32[2,32,128]{2,1,0:T(8,128)S(1)} %copy-done.7), channel_id=1, replica_groups=mesh['row'=16,'col'=16] {'row'}, dimensions={0}, use_global_device_ids=true | all-gather | bytes 557056 | tf_op jit(solution)/shard_map/all_gather | solution.py:56
  64.9 6.2 fusion.5
  71.1 4.7 scatter_fusion
  88.7 58.4 %all-reduce.7 = f32[32,1,128]{2,0,1:T(8,128)S(1)} all-reduce(f32[32,1,128]{2,0,1:T(8,128)S(1)} %bitcast.49), channel_id=9, replica_groups=mesh['row'=16,'col'=16] {'row'}, use_global_device_ids=true, to_apply=%region_5.7.clone | all-reduce | flops 4096 | bytes 32768
  147.2 61.3 %all-reduce.6 = f32[32,1,128]{2,0,1:T(8,128)S(1)} all-reduce(f32[32,1,128]{2,0,1:T(8,128)S(1)} %bitcast.48), channel_id=8, replica_groups=mesh['row'=16,'col'=16] {'col'}, use_global_device_ids=true, to_apply=%region_3.5.clone | all-reduce | flops 4096 | bytes 32768
  210.7 234.3 %all-reduce.11.cloned.1.call-done = (f32[8192]{0:T(1024)}, f32[8192]{0:T(1024)}) async-done(((f32[8192]{0:T(1024)}, f32[8192]{0:T(1024)}), (f32[8192]{0:T(1024)}, f32[8192]{0:T(1024)})) %all-reduce.11.cloned.1.call-update) | async-done | bytes 65552
  448.1 74.5 %all-reduce.2 = f32[8192]{0:T(1024)S(1)} all-reduce(f32[8192]{0:T(1024)S(1)} %dynamic-update-slice.2), channel_id=4, replica_groups=mesh['row'=16,'col'=16] {'row','col'}, use_global_device_ids=true, to_apply=%add.2 | all-reduce | flops 8192 | bytes 65536
  522.9 18.4 %all_gather.63 = f32[32,32,128]{2,1,0:T(8,128)S(1)} all-gather(f32[2,32,128]{2,1,0:T(8,128)S(1)} %multiply_add_fusion.4), channel_id=1, replica_groups=mesh['row'=16,'col'=16] {'col'}, dimensions={0}, use_global_device_ids=true | all-gather | bytes 557056 | tf_op jit(solution)/shard_map/all_gather | solution.py:55
  552.7 17.3 %all_gather.62 = f32[32,32,128]{2,1,0:T(8,128)S(1)} all-gather(f32[2,32,128]{2,1,0:T(8,128)S(1)} %multiply_add_fusion.4), channel_id=1, replica_groups=mesh['row'=16,'col'=16] {'row'}, dimensions={0}, use_global_device_ids=true | all-gather | bytes 557056 | tf_op jit(solution)/shard_map/all_gather | solution.py:56
  571.4 6.2 fusion.3
  577.6 4.7 scatter_fusion.2
  583.2 39.0 %reduce-scatter.15.cloned.1.call-done = f32[2,32,128]{2,1,0:T(8,128)} async-done(((f32[32,32,128]{2,1,0:T(8,128)}), f32[2,32,128]{2,1,0:T(8,128)}) %reduce-scatter.15.cloned.1.call-update) | async-done | bytes 32784 | tf_op jit(solution)/shard_map/reduce_scatter | solution.py:20
  622.3 57.2 %reduce-scatter.13.cloned.1.call-done = f32[2,32,128]{2,1,0:T(8,128)} async-done(((f32[32,32,128]{2,1,0:T(8,128)}), f32[2,32,128]{2,1,0:T(8,128)}) %reduce-scatter.13.cloned.1.call-update) | async-done | bytes 32784 | tf_op jit(solution)/shard_map/reduce_scatter | solution.py:20
  680.7 79.8 %all-reduce.3 = f32[8192]{0:T(1024)S(1)} all-reduce(f32[8192]{0:T(1024)S(1)} %dynamic-update-slice.3), channel_id=5, replica_groups=mesh['row'=16,'col'=16] {'row','col'}, use_global_device_ids=true, to_apply=%add.3 | all-reduce | flops 8192 | bytes 65536
  761.9 72.7 %all-reduce.4 = f32[8192]{0:T(1024)S(1)} all-reduce(f32[8192]{0:T(1024)S(1)} %dynamic-update-slice.4), channel_id=6, replica_groups=mesh['row'=16,'col'=16] {'row','col'}, use_global_device_ids=true, to_apply=%add.4 | all-reduce | flops 8192 | bytes 65536
  834.8 18.1 %all_gather.69 = f32[32,32,128]{2,1,0:T(8,128)S(1)} all-gather(f32[2,32,128]{2,1,0:T(8,128)S(1)} %multiply_add_fusion.2), channel_id=1, replica_groups=mesh['row'=16,'col'=16] {'col'}, dimensions={0}, use_global_device_ids=true | all-gather | bytes 557056 | tf_op jit(solution)/shard_map/all_gather | solution.py:55
  864.3 18.5 %all_gather.68 = f32[32,32,128]{2,1,0:T(8,128)S(1)} all-gather(f32[2,32,128]{2,1,0:T(8,128)S(1)} %multiply_add_fusion.2), channel_id=1, replica_groups=mesh['row'=16,'col'=16] {'row'}, dimensions={0}, use_global_device_ids=true | all-gather | bytes 557056 | tf_op jit(solution)/shard_map/all_gather | solution.py:56
  884.3 5.3 fusion.1
  893.2 42.4 %reduce-scatter.19.cloned.1.call-done = f32[2,32,128]{2,1,0:T(8,128)} async-done(((f32[32,32,128]{2,1,0:T(8,128)}), f32[2,32,128]{2,1,0:T(8,128)}) %reduce-scatter.19.cloned.1.call-update) | async-done | bytes 32784 | tf_op jit(solution)/shard_map/reduce_scatter | solution.py:20
  935.5 57.4 %reduce-scatter.17.cloned.1.call-done = f32[2,32,128]{2,1,0:T(8,128)} async-done(((f32[32,32,128]{2,1,0:T(8,128)}), f32[2,32,128]{2,1,0:T(8,128)}) %reduce-scatter.17.cloned.1.call-update) | async-done | bytes 32784 | tf_op jit(solution)/shard_map/reduce_scatter | solution.py:20
  994.1 79.8 %all-reduce.5 = f32[8192]{0:T(1024)S(1)} all-reduce(f32[8192]{0:T(1024)S(1)} %dynamic-update-slice.5), channel_id=7, replica_groups=mesh['row'=16,'col'=16] {'row','col'}, use_global_device_ids=true, to_apply=%add.5 | all-reduce | flops 8192 | bytes 65536
  (112 shorter events, 57.3 us)
Async XLA Ops:
  7.2 201.3 %reduce-scatter.11.cloned.1.call-start = ((), (), s32[]{:S(2)}) async-start(), calls=%async_computation.7 | async-start | bytes 557056 | tf_op jit(solution)/shard_map/reduce_scatter | solution.py:20
  33.0 10.9 %copy-start.7 = (f32[2,32,128]{2,1,0:T(8,128)S(1)}, f32[2,32,128]{2,1,0:T(8,128)}, u32[]{:S(2)}) copy-start(f32[2,32,128]{2,1,0:T(8,128)} %param.13) | copy-start | bytes 98308
  38.0 26.9 %copy-start = (f32[1,1,40,128,128]{4,3,2,1,0:T(8,128)S(1)}, f32[1,1,40,128,128]{4,3,2,1,0:T(8,128)}, u32[]{:S(2)}) copy-start(f32[1,1,40,128,128]{4,3,2,1,0:T(8,128)} %param.9) | copy-start | bytes 7864324
  42.9 0.8 copy-start.3
  43.8 164.7 %reduce-scatter.9.cloned.1.call-start = ((), (), s32[]{:S(2)}) async-start(), calls=%async_computation.6 | async-start | bytes 557056 | tf_op jit(solution)/shard_map/reduce_scatter | solution.py:20
  71.1 6.8 copy-start.12
  71.1 7.4 copy-start.11
  75.8 0.8 copy-start.4
  76.7 368.4 %all-reduce.11.cloned.1.call-start = ((), (), s32[]{:S(2)}) async-start(), calls=%async_computation.12 | async-start | bytes 131072
  80.5 128.1 %copy-start.10 = (f32[32]{0:T(128)S(1)}, f32[32]{0:T(128)}, u32[]{:S(2)}) copy-start(f32[32]{0:T(128)} %param.12) | copy-start | bytes 388
  209.8 0.6 copy-start.8
  210.0 0.6 copy-start.9
  210.7 411.6 %reduce-scatter.15.cloned.1.call-start = ((), (), s32[]{:S(2)}) async-start(), calls=%async_computation.9 | async-start | bytes 557056 | tf_op jit(solution)/shard_map/reduce_scatter | solution.py:20
  551.8 0.8 copy-start.5
  552.6 126.8 %reduce-scatter.13.cloned.1.call-start = ((), (), s32[]{:S(2)}) async-start(), calls=%async_computation.8 | async-start | bytes 557056 | tf_op jit(solution)/shard_map/reduce_scatter | solution.py:20
  582.4 0.8 copy-start.6
  583.2 352.4 %reduce-scatter.19.cloned.1.call-start = ((), (), s32[]{:S(2)}) async-start(), calls=%async_computation.11 | async-start | bytes 557056 | tf_op jit(solution)/shard_map/reduce_scatter | solution.py:20
  863.5 0.8 copy-start.1
  864.3 128.6 %reduce-scatter.17.cloned.1.call-start = ((), (), s32[]{:S(2)}) async-start(), calls=%async_computation.10 | async-start | bytes 557056 | tf_op jit(solution)/shard_map/reduce_scatter | solution.py:20
  892.3 0.8 copy-start.2
Sparse Core Ops, SparseCore 0:
  43.9 73.3 reduce-scatter.10
  120.0 55.2 reduce-scatter.8
  210.8 234.2 all-reduce.10
  552.7 69.4 reduce-scatter.14
  624.8 54.6 reduce-scatter.12
  864.4 71.0 reduce-scatter.18
  938.2 54.6 reduce-scatter.16
